TPU v7x, 256 devices: a whole 4x4x8 slice. The times are simulated.
256 devices in a mesh: ka: 32 (over y, z_hi, x), occ: 8 (over z_lo, core).
Axes of the slice: x: 4, y: 4, z: 8 (z_hi: 2, z_lo: 4; z = z_hi * 4 + z_lo), core: 2. Of those that a mesh axis runs over, the one named last changes fastest.
Arguments:
- factors: bfloat16 [64, 8, 192, 2, 768], P('ka'), may hold values from -0.23925781 to 0.23925781
- occupied_energy: float32 [8], replicated, may hold values from -2 to -0.5
- virtual_energy: bfloat16 [64, 192], P('ka'), may hold values from 0.5 to 3
- conserve: int32 [64, 2], P('ka'), may hold values from 0 to 63, as said below
- pair_lists: int32 [2, 16, 2], P(None, 'occ'), may hold values from 0 to 7, as said below
Outputs:
- density: float32 [64, 192, 2, 192], P('ka', 'occ')
Inputs may be any that keep to these rules, and one draw needn't show every extreme that they name: For a momentum ka among the 2 momenta of block d (momenta d * 2 to d * 2 + 1), (64 - conserve[ka, r]) mod 64 lies in block (d - r - 1) mod 32; the 2 momenta of one block name different momenta in each round. `pair_lists`: each entry is an ordered pair (i, j) of occupied orbitals; every round begins with the pairs (0, 0) and (7, 7); within a round no ordered pair repeats (16 of the 64 ordered pairs appear).
All inputs are finite; a program needn't handle non-finite values.
Results may differ from a plain program's by a relative error of at most 0.00082.
Values may be sent and summed in bfloat16 or wider, within the bound.
No kernel may reach another device: no remote copies, remote signals or barrier semaphores. Data moves between devices by JAX's collectives and lax.ppermute only.
A program may use at most 128 MiB of HBM per device.

v0:
```python
import jax
import jax.numpy as jnp
from jax import lax
from jax.sharding import PartitionSpec as P


def from_behind(array, axis, by):
    size = lax.axis_size(axis)
    return lax.ppermute(array, axis, [(i, (i + by) % size) for i in range(size)])


def cut_along(array, dim, size):
    before, after = (array.shape[:dim], array.shape[dim + 1 :])
    return jnp.moveaxis(array.reshape(*before, size, -1, *after), dim, 0)


def sent_and_summed(array, axis, dim):
    size = lax.axis_size(axis)
    parts = lax.all_to_all(cut_along(array, dim, size), axis, 0, 0, tiled=True)
    return jnp.sum(parts, axis=0)


def build_mates(received, auxiliary):
    real_part = received[..., :auxiliary]
    imaginary = received[..., auxiliary:]
    turned = jnp.concatenate([-imaginary, real_part], axis=-1)
    return jnp.concatenate([received, turned], axis=-2)


def amplitude(left_rows, mate_rows, energy_left, energy_right, occupied_sum):
    values = lax.dot_general(
        left_rows, mate_rows, (((1,), (1,)), ((), ())), preferred_element_type=jnp.float32
    )
    denominator = energy_left[:, None] + energy_right[None, :] - occupied_sum
    return values / jnp.concatenate([denominator, denominator], axis=1)


def density_term(amplitudes, swapped):
    virtuals = amplitudes.shape[0]
    combined = (2.0 * amplitudes - swapped).astype(jnp.bfloat16)
    rounded = amplitudes.astype(jnp.bfloat16)
    turned = jnp.concatenate([-rounded[:, virtuals:], rounded[:, :virtuals]], axis=1)
    stacked = jnp.concatenate([rounded, turned], axis=0)
    return lax.dot_general(
        combined, stacked, (((1,), (1,)), ((), ())), preferred_element_type=jnp.float32
    )


def pair_term(own_block, mate_block, energy_left, energy_right, occupied_energy, pair_row):
    leading = pair_row[0]
    trailing = pair_row[1]
    occupied_sum = occupied_energy[leading] + occupied_energy[trailing]
    amplitudes = amplitude(
        own_block[leading], mate_block[trailing], energy_left, energy_right, occupied_sum
    )
    swapped = amplitude(
        own_block[trailing], mate_block[leading], energy_left, energy_right, occupied_sum
    )
    return density_term(amplitudes, swapped)


def local(factors, occupied_energy, virtual_energy, conserve, pair_lists):
    momenta = factors.shape[0]
    orbitals = factors.shape[1]
    virtuals = factors.shape[2]
    auxiliary = factors.shape[4]
    own = factors.reshape(momenta, orbitals, virtuals, 2 * auxiliary)
    energy_own = virtual_energy.astype(jnp.float32)
    density = jnp.zeros((momenta, virtuals, 2 * virtuals), jnp.float32)
    for round_index in range(conserve.shape[1]):
        portion = orbitals // lax.axis_size("occ")
        portion_block = lax.dynamic_slice_in_dim(
            factors, lax.axis_index("occ") * portion, portion, 1
        )
        shifted, energy_mate = from_behind((portion_block, virtual_energy), "ka", round_index + 1)
        received = lax.all_gather(shifted, "occ", axis=1, tiled=True)
        mates = build_mates(received.reshape(momenta, orbitals, virtuals, 2 * auxiliary), auxiliary)
        energy_mate = energy_mate.astype(jnp.float32)
        for local_index in range(momenta):
            chosen = (momenta - conserve[local_index, round_index] % momenta) % momenta
            mate_block = lax.dynamic_index_in_dim(mates, chosen, 0, keepdims=False)
            energy_right = lax.dynamic_index_in_dim(energy_mate, chosen, 0, keepdims=False)
            own_block = own[local_index]
            energy_left = energy_own[local_index]

            def add_pair(partial_sum, pair_row):
                term = pair_term(
                    own_block, mate_block, energy_left, energy_right, occupied_energy, pair_row
                )
                return (partial_sum + term, None)

            running, ignored = lax.scan(add_pair, density[local_index], pair_lists[round_index])
            density = density.at[local_index].set(running)
    shaped = density.reshape(momenta, virtuals, 2, virtuals)
    return sent_and_summed(shaped, "occ", 1)


def solution(mesh):
    in_specs = (
        P("ka", None, None, None, None),
        P(),
        P("ka", None),
        P("ka", None),
        P(None, "occ", None),
    )
    out_specs = P("ka", "occ", None, None)
    return jax.shard_map(local, mesh=mesh, in_specs=in_specs, out_specs=out_specs, check_vma=False)
```

profile of v0, /device:TPU:1, one launch (start us, length us, event | category | flops | bytes accessed | tf_op | source)
XLA Modules:
  0.0 440.6 jit_solution(3128078142213431730)
XLA Ops:
  6.5 2.1 constant_dynamic-slice_fusion.8
  8.6 2.1 collective-permute-start
  10.7 43.4 %collective-permute-done = bf16[2,1,192,2,768]{4,3,2,1,0:T(2,128)(2,1)S(1)} collective-permute-done((bf16[2,1,192,2,768]{4,3,2,1,0:T(2,128)(2,1)S(1)}, bf16[2,1,192,2,768]{4,3,2,1,0:T(2,128)(2,1)S(1)}, u32[]{:S(2)}, u32[]{:S(2)}) %collective-permute-start) | collective-permute-done | bytes 1179680 | tf_op jit(solution)/shard_map/ppermute | solution.py:9
  54.2 1.0 copy-done.3
  55.4 33.9 %collective-permute-done.2 = bf16[2,1,192,2,768]{4,3,2,1,0:T(2,128)(2,1)S(1)} collective-permute-done((bf16[2,1,192,2,768]{4,3,2,1,0:T(2,128)(2,1)S(1)}, bf16[2,1,192,2,768]{4,3,2,1,0:T(2,128)(2,1)S(1)}, u32[]{:S(2)}, u32[]{:S(2)}) %collective-permute-start.2) | collective-permute-done | bytes 1179680 | tf_op jit(solution)/shard_map/ppermute | solution.py:9
  89.2 1.0 copy-done.2
  90.4 11.3 %collective-permute-start.3 = (bf16[2,192]{1,0:T(2,128)(2,1)}, bf16[2,192]{1,0:T(2,128)(2,1)S(1)}, u32[]{:S(2)}, u32[]{:S(2)}) collective-permute-start(bf16[2,192]{1,0:T(2,128)(2,1)} %param.23), channel_id=1, source_target_pairs={{0,16},{8,24},{16,32},{24,40},{32,48},{40,56},{48,64},{56,72},{64,... | collective-permute-start | bytes 2312 | tf_op jit(solution)/shard_map/ppermute | solution.py:9
  101.6 1.5 fusion.169
  111.1 0.8 fusion.170
  111.9 0.7 slice_bitcast_fusion.1
  112.6 9.8 %fusion.168 = (bf16[1,8,192,2,768]{4,3,2,1,0:T(2,128)(2,1)}, bf16[1,8,192,2,768]{4,3,2,1,0:T(2,128)(2,1)}) fusion(bf16[2,8,192,2,768]{4,3,2,1,0:T(2,128)(2,1)} %param.21), kind=kLoop, calls=%fused_computation.155 | loop fusion | bytes 18874368 | tf_op jit(solution)/shard_map/slice | solution.py:83
  122.4 11.3 %squeeze.153 = bf16[8,192,1536]{2,1,0:T(8,128)(2,1)} reshape(bf16[1,8,192,2,768]{4,3,2,1,0:T(2,128)(2,1)} %get-tuple-element.382) | data formatting | bytes 9437184 | tf_op jit(solution)/shard_map/squeeze | solution.py:83
  133.7 11.3 %squeeze.149 = bf16[8,192,1536]{2,1,0:T(8,128)(2,1)} reshape(bf16[1,8,192,2,768]{4,3,2,1,0:T(2,128)(2,1)} %get-tuple-element.381) | data formatting | bytes 9437184 | tf_op jit(solution)/shard_map/squeeze | solution.py:83
  145.0 50.5 %all-gather.3.cloned.1.call-done = bf16[2,8,192,2,768]{4,3,2,1,0:T(2,128)(2,1)} async-done(((bf16[2,1,192,2,768]{4,3,2,1,0:T(2,128)(2,1)}), bf16[2,8,192,2,768]{4,3,2,1,0:T(2,128)(2,1)}) %all-gather.3.cloned.1.call-update) | async-done | bytes 9437200 | tf_op jit(solution)/shard_map/all_gather | solution.py:76
  195.5 20.9 %reshape.159 = bf16[2,8,192,1536]{3,2,1,0:T(8,128)(2,1)} reshape(bf16[2,8,192,2,768]{4,3,2,1,0:T(2,128)(2,1)} %all-gather.3.cloned.1.call-done) | data formatting | bytes 18874368 | tf_op jit(solution)/shard_map/reshape | solution.py:77
  216.3 8.6 %slice_negate_fusion.5 = (bf16[2,8,192,768]{3,2,1,0:T(8,128)(2,1)}, bf16[2,8,192,768]{3,2,1,0:T(8,128)(2,1)}) fusion(bf16[2,8,192,1536]{3,2,1,0:T(8,128)(2,1)} %reshape.159), kind=kLoop, calls=%fused_computation.131 | loop fusion | flops 2359296 | bytes 18874368 | tf_op jit(solution)/shard_map/neg | solution.py:26
  225.0 6.3 %maximum_maximum_fusion = bf16[2,8,384,1536]{3,2,1,0:T(8,128)(2,1)S(1)} fusion(bf16[2,8,192,768]{3,2,1,0:T(8,128)(2,1)} %get-tuple-element.384, bf16[2,8,192,768]{3,2,1,0:T(8,128)(2,1)} %get-tuple-element.383, bf16[2,8,192,1536]{3,2,1,0:T(8,128)(2,1)S(1)} %copy-done), kind=kLoop, calls=%fused_computation.124 | loop fusion | flops 56623104 | bytes 37748736 | tf_op jit(solution)/shard_map/concatenate | solution.py:27
  231.4 6.9 %dynamic-slice_bitcast_fusion.3 = (bf16[8,384,1536]{2,1,0:T(8,128)(2,1)}, bf16[8,384,1536]{2,1,0:T(8,128)(2,1)}) fusion(bf16[2,8,384,1536]{3,2,1,0:T(8,128)(2,1)S(1)} %maximum_maximum_fusion, s32[]{:T(128)S(6)} %select_n.100, s32[]{:T(128)S(6)} %select_n.103), kind=kLoop, calls=%fused_computation.129 | loop fusion | bytes 37748744 | tf_op jit(solution)/shard_map/jit(dynamic_index_in_dim)/squeeze | solution.py:81
  238.3 21.6 %while.48 = (s32[]{:T(128)}, f32[192,384]{1,0:T(8,128)S(1)}, s32[2,2]{1,0:T(2,128)S(1)}, bf16[8,192,1536]{2,1,0:T(8,128)(2,1)}, bf16[8,384,1536]{2,1,0:T(8,128)(...) while((s32[]{:T(128)}, f32[192,384]{1,0:T(8,128)S(1)}, ...), condition=%wide.region_1.2_spmd.clone, body=%wide.region_0.1_spmd.clone.sunk | while | flops 511340544 | bytes 5900063 | solution.py:92
  238.3 0.6 fusion.210
  242.6 0.7 fusion.211
  244.5 2.0 fusion.212
  246.7 2.4 convolution_add_fusion.10
  249.1 0.6 fusion.210
  253.4 0.7 fusion.211
  255.3 2.0 fusion.212
  257.5 2.3 convolution_add_fusion.10
  259.8 0.7 copy-done.4
  260.5 1.0 copy.20
  261.5 21.6 %while.49 = (s32[]{:T(128)}, f32[192,384]{1,0:T(8,128)S(1)}, s32[2,2]{1,0:T(2,128)S(1)}, bf16[8,192,1536]{2,1,0:T(8,128)(2,1)}, bf16[8,384,1536]{2,1,0:T(8,128)(...) while((s32[]{:T(128)}, f32[192,384]{1,0:T(8,128)S(1)}, ...), condition=%wide.region_3.4_spmd.clone, body=%wide.region_2.3_spmd.clone.sunk | while | flops 511340544 | bytes 5900063 | solution.py:92
  261.5 0.6 fusion.216
  265.8 0.7 fusion.217
  267.8 2.0 fusion.218
  269.9 2.3 convolution_add_fusion.11
  272.3 0.6 fusion.216
  276.6 0.7 fusion.217
  278.6 2.0 fusion.218
  280.7 2.3 convolution_add_fusion.11
  283.1 36.5 %all-gather.5.cloned.1.call-done = bf16[2,8,192,2,768]{4,3,2,1,0:T(2,128)(2,1)} async-done(((bf16[2,1,192,2,768]{4,3,2,1,0:T(2,128)(2,1)}), bf16[2,8,192,2,768]{4,3,2,1,0:T(2,128)(2,1)}) %all-gather.5.cloned.1.call-update) | async-done | bytes 9437200 | tf_op jit(solution)/shard_map/all_gather | solution.py:76
  319.6 20.9 %reshape.161 = bf16[2,8,192,1536]{3,2,1,0:T(8,128)(2,1)} reshape(bf16[2,8,192,2,768]{4,3,2,1,0:T(2,128)(2,1)} %all-gather.5.cloned.1.call-done) | data formatting | bytes 18874368 | tf_op jit(solution)/shard_map/reshape | solution.py:77
  340.5 8.6 %slice_negate_fusion.4 = (bf16[2,8,192,768]{3,2,1,0:T(8,128)(2,1)}, bf16[2,8,192,768]{3,2,1,0:T(8,128)(2,1)}) fusion(bf16[2,8,192,1536]{3,2,1,0:T(8,128)(2,1)} %reshape.161), kind=kLoop, calls=%fused_computation.130 | loop fusion | flops 2359296 | bytes 18874368 | tf_op jit(solution)/shard_map/neg | solution.py:26
  349.1 6.3 %maximum_maximum_fusion.1 = bf16[2,8,384,1536]{3,2,1,0:T(8,128)(2,1)S(1)} fusion(bf16[2,8,192,768]{3,2,1,0:T(8,128)(2,1)} %get-tuple-element.380, bf16[2,8,192,768]{3,2,1,0:T(8,128)(2,1)} %get-tuple-element.379, bf16[2,8,192,1536]{3,2,1,0:T(8,128)(2,1)S(1)} %copy-done.1), kind=kLoop, calls=%fused_computation.125 | loop fusion | flops 56623104 | bytes 37748736 | tf_op jit(solution)/shard_map/concatenate | solution.py:27
  355.5 6.9 %dynamic-slice_bitcast_fusion = (bf16[8,384,1536]{2,1,0:T(8,128)(2,1)}, bf16[8,384,1536]{2,1,0:T(8,128)(2,1)}) fusion(bf16[2,8,384,1536]{3,2,1,0:T(8,128)(2,1)S(1)} %maximum_maximum_fusion.1, s32[]{:T(128)S(6)} %select_n.109, s32[]{:T(128)S(6)} %select_n.106), kind=kLoop, calls=%fused_computation.126 | loop fusion | bytes 37748744 | tf_op jit(solution)/shard_map/jit(dynamic_index_in_dim)/squeeze | solution.py:81
  362.4 21.7 %while.46 = (s32[]{:T(128)}, f32[192,384]{1,0:T(8,128)S(1)}, s32[2,2]{1,0:T(2,128)S(1)}, bf16[8,192,1536]{2,1,0:T(8,128)(2,1)}, bf16[8,384,1536]{2,1,0:T(8,128)(...) while((s32[]{:T(128)}, f32[192,384]{1,0:T(8,128)S(1)}, ...), condition=%wide.region_5.6_spmd, body=%wide.region_4.5_spmd.sunk | while | flops 511266816 | bytes 5900053 | solution.py:92
  362.4 0.6 fusion.198
  366.8 0.6 fusion.199
  368.8 2.0 fusion.200
  371.0 2.3 convolution_add_fusion.8
  373.3 0.6 fusion.198
  377.7 0.6 fusion.199
  379.7 2.0 fusion.200
  381.8 2.3 convolution_add_fusion.8
  384.2 22.2 %while.47 = (s32[]{:T(128)}, f32[192,384]{1,0:T(8,128)S(1)}, s32[2,2]{1,0:T(2,128)S(1)}, bf16[8,192,1536]{2,1,0:T(8,128)(2,1)}, bf16[8,384,1536]{2,1,0:T(8,128)(...) while((s32[]{:T(128)}, f32[192,384]{1,0:T(8,128)S(1)}, ...), condition=%wide.region_7.8_spmd, body=%wide.region_6.7_spmd.sunk | while | flops 511266816 | bytes 5900053 | solution.py:92
  384.3 0.6 fusion.204
  388.8 0.7 fusion.205
  390.9 2.0 fusion.206
  393.0 2.3 convolution_add_fusion.9
  395.4 0.6 fusion.204
  399.9 0.7 fusion.205
  402.0 2.0 fusion.206
  404.1 2.3 convolution_add_fusion.9
  406.4 0.6 reshape_reshape.3
  407.3 25.4 %all_to_all.5 = f32[8,2,24,2,192]{4,3,2,1,0:T(2,128)S(1)} all-to-all(f32[8,2,24,2,192]{4,3,2,1,0:T(2,128)S(1)} %copy.6), channel_id=1, replica_groups=mesh['ka'=32,'occ'=8] {'occ'}, dimensions={0} | all-to-all | bytes 1179648 | tf_op jit(solution)/shard_map/all_to_all | solution.py:19
  432.7 1.0 reduce_sum.9
  (60 shorter events, 2.4 us)
Async XLA Ops:
  6.5 188.9 %all-gather.3.cloned.1.call-start = ((), (), s32[]{:S(2)}) async-start(), calls=%async_computation.1 | async-start | bytes 10616832 | tf_op jit(solution)/shard_map/all_gather | solution.py:76
  8.6 45.5 %collective-permute-start = (bf16[2,1,192,2,768]{4,3,2,1,0:T(2,128)(2,1)S(1)}, bf16[2,1,192,2,768]{4,3,2,1,0:T(2,128)(2,1)S(1)}, u32[]{:S(2)}, u32[]{:S(2)}) collective-permute-start(bf16[2,1,192,2,768]{4,3,2,1,0:T(2,128)(2,1)S(1)} %constant_dynamic-slice_fusion.8), channel_id=1, source_target_pairs={{0,8},{8,16},{16,24},{24,32},{32,40},{40,48},{48,56},{56,64},{64,7... | collective-permute-start | bytes 3538952 | tf_op jit(solution)/shard_map/ppermute | solution.py:9
  54.2 1.0 copy-start.3
  55.2 264.4 %all-gather.5.cloned.1.call-start = ((), (), s32[]{:S(2)}) async-start(), calls=%async_computation.2 | async-start | bytes 10616832 | tf_op jit(solution)/shard_map/all_gather | solution.py:76
  55.3 34.0 %collective-permute-start.2 = (bf16[2,1,192,2,768]{4,3,2,1,0:T(2,128)(2,1)S(1)}, bf16[2,1,192,2,768]{4,3,2,1,0:T(2,128)(2,1)S(1)}, u32[]{:S(2)}, u32[]{:S(2)}) collective-permute-start(bf16[2,1,192,2,768]{4,3,2,1,0:T(2,128)(2,1)S(1)} %constant_dynamic-slice_fusion.8), channel_id=1, source_target_pairs={{0,16},{8,24},{16,32},{24,40},{32,48},{40,56},{48,64},{56,72},{64,... | collective-permute-start | bytes 3538952 | tf_op jit(solution)/shard_map/ppermute | solution.py:9
  89.2 1.0 copy-start.2
  90.3 54.7 %collective-permute-start.1 = (bf16[2,192]{1,0:T(2,128)(2,1)}, bf16[2,192]{1,0:T(2,128)(2,1)S(1)}, u32[]{:S(2)}, u32[]{:S(2)}) collective-permute-start(bf16[2,192]{1,0:T(2,128)(2,1)} %param.23), channel_id=1, source_target_pairs={{0,8},{8,16},{16,24},{24,32},{32,40},{40,48},{48,56},{56,64},{64,7... | collective-permute-start | bytes 2312 | tf_op jit(solution)/shard_map/ppermute | solution.py:9
  90.4 54.6 %collective-permute-start.3 = (bf16[2,192]{1,0:T(2,128)(2,1)}, bf16[2,192]{1,0:T(2,128)(2,1)S(1)}, u32[]{:S(2)}, u32[]{:S(2)}) collective-permute-start(bf16[2,192]{1,0:T(2,128)(2,1)} %param.23), channel_id=1, source_target_pairs={{0,16},{8,24},{16,32},{24,40},{32,48},{40,56},{48,64},{56,72},{64,... | collective-permute-start | bytes 2312 | tf_op jit(solution)/shard_map/ppermute | solution.py:9
  216.3 8.7 %copy-start = (bf16[2,8,192,1536]{3,2,1,0:T(8,128)(2,1)S(1)}, bf16[2,8,192,1536]{3,2,1,0:T(8,128)(2,1)}, u32[]{:S(2)}) copy-start(bf16[2,8,192,1536]{3,2,1,0:T(8,128)(2,1)} %reshape.159) | copy-start | bytes 28311556
  231.4 6.9 %copy-start.6 = (f32[8]{0:T(128)S(1)}, f32[8]{0:T(128)}, u32[]{:S(2)}) copy-start(f32[8]{0:T(128)} %param.22) | copy-start | bytes 100
  238.2 23.2 %copy-start.7 = (f32[192,384]{1,0:T(8,128)S(1)}, f32[192,384]{1,0:T(8,128)}, u32[]{:S(2)}) copy-start(f32[192,384]{1,0:T(8,128)} %custom-call.1) | copy-start | bytes 884740
  259.8 0.7 copy-start.4
  283.1 36.5 %copy-start.8 = (f32[192,384]{1,0:T(8,128)}, f32[192,384]{1,0:T(8,128)S(1)}, u32[]{:S(2)}) copy-start(f32[192,384]{1,0:T(8,128)S(1)} %get-tuple-element.222) | copy-start | bytes 884740
  340.5 8.7 %copy-start.1 = (bf16[2,8,192,1536]{3,2,1,0:T(8,128)(2,1)S(1)}, bf16[2,8,192,1536]{3,2,1,0:T(8,128)(2,1)}, u32[]{:S(2)}) copy-start(bf16[2,8,192,1536]{3,2,1,0:T(8,128)(2,1)} %reshape.161) | copy-start | bytes 28311556
  362.4 21.7 %copy-start.5 = (f32[192,384]{1,0:T(8,128)S(1)}, f32[192,384]{1,0:T(8,128)}, u32[]{:S(2)}) copy-start(f32[192,384]{1,0:T(8,128)} %copy-done.4) | copy-start | bytes 884740
  362.4 21.7 %copy-start.9 = (f32[192,384]{1,0:T(8,128)S(1)}, f32[192,384]{1,0:T(8,128)}, u32[]{:S(2)}) copy-start(f32[192,384]{1,0:T(8,128)} %copy-done.8) | copy-start | bytes 884740
Sparse Core Ops, SparseCore 0:
  55.3 140.0 all-gather.2
  197.3 122.2 all-gather.4
where the time goes:
time: 444 us; the launch traced here: 441 us
  waiting for transfers between devices  164 us (37%)
  local copies, waits for them, and re-layouts  108 us (24%)
  loops' own time  40.8 us (9%)
  matrix products  34.6 us (8%)
  other arithmetic  32.5 us (7%)
  blocking collectives  25.4 us (6%)
  between operations  21.6 us (5%)
  starting transfers between devices  13.6 us (3%)
    all_gather x2, waiting for transfers between devices, local(): received = lax.all_gather(shifted, 'occ', axis=1, tiled=True)  87 us
    ppermute x4, waiting for transfers between devices, from_behind(): lax.ppermute(array, axis, [(i, (i + by) % size) for i in range(size)])  77.3 us
    reshape x2, local copies, waits for them, and re-layouts, local(): received.reshape(momenta, orbitals, virtuals, 2 * auxiliary)  41.7 us
    another operation x4, loops' own time, local(): lax.scan(add_pair, density[local_index], pair_lists[round_index])  40.8 us
    all_to_all x1, blocking collectives, sent_and_summed(): parts = lax.all_to_all(cut_along(array, dim, size), axis, 0, 0, tiled=True)  25.4 us
    squeeze x2, local copies, waits for them, and re-layouts, local(): own_block = own[local_index]  22.6 us
    dot_general x8, matrix products, density_term(): lax.dot_general(combined, stacked, (((1,), (1,)), ((), ())), preferred_el...  18.4 us
    neg x2, other arithmetic, build_mates(): turned = jnp.concatenate([-imaginary, real_part], axis=-1)  17.2 us
  transfers between devices with their start and end apart: 6, of which 4 were waited for; matrix products, arithmetic and copies ran while one was open for 23% of the time, Pallas kernels for 0%

commit v1 on v0

--- a/solution.py
+++ b/solution.py
@@ -73,7 +73,9 @@
             factors, lax.axis_index("occ") * portion, portion, 1
         )
         shifted, energy_mate = from_behind((portion_block, virtual_energy), "ka", round_index + 1)
-        received = lax.all_gather(shifted, "occ", axis=1, tiled=True)
+        received = jnp.concatenate(
+            lax.all_to_all(jnp.stack([shifted] * lax.axis_size("occ")), "occ", 0, 0), axis=1
+        )
         mates = build_mates(received.reshape(momenta, orbitals, virtuals, 2 * auxiliary), auxiliary)
         energy_mate = energy_mate.astype(jnp.float32)
         for local_index in range(momenta):

time: 444 us -> 702 us (1.58)
  waiting for transfers between devices: 164 us -> 359 us
  starting transfers between devices: 13.6 us -> 81.6 us
  between operations: 21.6 us -> 7.74 us
  local copies, waits for them, and re-layouts: 108 us -> 116 us
    ppermute x4, waiting for transfers between devices: 77.3 us -> 336 us  [from_behind(): lax.ppermute(array, axis, [(i, (i + by) % size) for i in range(size)])]
    all_gather x2 -> x0, waiting for transfers between devices: 87 us -> none  [local(): received = lax.all_gather(shifted, 'occ', axis=1, tiled=True)]
    another operation x0 -> x4, local copies, waits for them, and re-layouts: none -> 54.1 us  [the longest x2 41.8 us: local(): received.reshape(momenta, orbitals, virtuals, 2 * auxiliary)]
    reshape x2 -> x0, local copies, waits for them, and re-layouts: 41.7 us -> none  [local(): received.reshape(momenta, orbitals, virtuals, 2 * auxiliary)]
    ppermute x4, starting transfers between devices: 13.6 us -> 53 us  [from_behind(): lax.ppermute(array, axis, [(i, (i + by) % size) for i in range(size)])]
    all_to_all x0 -> x2, starting transfers between devices: none -> 28.5 us  [local(): lax.all_to_all(jnp.stack([shifted] * lax.axis_size('occ')), 'occ', 0, 0)]
    all_to_all x0 -> x2, waiting for transfers between devices: none -> 23.1 us  [local(): lax.all_to_all(jnp.stack([shifted] * lax.axis_size('occ')), 'occ', 0, 0)]
  transfers between devices with their start and end apart: 6 -> 6, of which waited for: 4 -> 4; matrix products, arithmetic and copies ran while one was open for 23% -> 14% of each run, Pallas kernels for 0% -> 0%
where the time goes in v1:
time: 702 us; the launch traced here: 698 us
  waiting for transfers between devices  359 us (51%)
  local copies, waits for them, and re-layouts  116 us (17%)
  starting transfers between devices  81.6 us (12%)
  loops' own time  40.9 us (6%)
  matrix products  34.5 us (5%)
  other arithmetic  32.4 us (5%)
  blocking collectives  25.5 us (4%)
  between operations  7.74 us (1%)
    ppermute x4, waiting for transfers between devices, from_behind(): lax.ppermute(array, axis, [(i, (i + by) % size) for i in range(size)])  336 us
    ppermute x4, starting transfers between devices, from_behind(): lax.ppermute(array, axis, [(i, (i + by) % size) for i in range(size)])  53 us
    another operation x2, local copies, waits for them, and re-layouts, local(): received.reshape(momenta, orbitals, virtuals, 2 * auxiliary)  41.8 us
    another operation x4, loops' own time, local(): lax.scan(add_pair, density[local_index], pair_lists[round_index])  40.9 us
    all_to_all x2, starting transfers between devices, local(): lax.all_to_all(jnp.stack([shifted] * lax.axis_size('occ')), 'occ', 0, 0)  28.5 us
    all_to_all x1, blocking collectives, sent_and_summed(): parts = lax.all_to_all(cut_along(array, dim, size), axis, 0, 0, tiled=True)  25.5 us
    all_to_all x2, waiting for transfers between devices, local(): lax.all_to_all(jnp.stack([shifted] * lax.axis_size('occ')), 'occ', 0, 0)  23.1 us
    squeeze x2, local copies, waits for them, and re-layouts, local(): own_block = own[local_index]  22.5 us
  transfers between devices with their start and end apart: 6, of which 4 were waited for; matrix products, arithmetic and copies ran while one was open for 14% of the time, Pallas kernels for 0%

profile of v1, /device:TPU:1, one launch (start us, length us, event | category | flops | bytes accessed | tf_op | source)
XLA Modules:
  0.0 698.2 jit_solution(11475505039707726185)
XLA Ops:
  0.0 2.1 constant_dynamic-slice_fusion.8
  2.1 2.1 collective-permute-start
  4.2 43.4 %collective-permute-done = bf16[2,1,192,2,768]{4,3,2,1,0:T(2,128)(2,1)S(1)} collective-permute-done((bf16[2,1,192,2,768]{4,3,2,1,0:T(2,128)(2,1)S(1)}, bf16[2,1,192,2,768]{4,3,2,1,0:T(2,128)(2,1)S(1)}, u32[]{:S(2)}, u32[]{:S(2)}) %collective-permute-start) | collective-permute-done | bytes 1179680 | tf_op jit(solution)/shard_map/ppermute | solution.py:9
  47.6 6.2 stack.4
  53.8 22.0 %all-to-all-start = ((bf16[8,2,1,192,2,768]{5,4,3,1,2,0:T(2,128)(2,1)}), bf16[8,2,1,192,2,768]{5,4,3,1,2,0:T(2,128)(2,1)}, u32[]{:S(2)}, u32[]{:S(2)}) async-start(bf16[8,2,1,192,2,768]{5,4,3,1,2,0:T(2,128)(2,1)} %stack.4), calls=%async_computation | async-start | bytes 18874368 | tf_op jit(solution)/shard_map/all_to_all | solution.py:77
  75.8 181.9 %collective-permute-done.2 = bf16[2,1,192,2,768]{4,3,2,1,0:T(2,128)(2,1)S(1)} collective-permute-done((bf16[2,1,192,2,768]{4,3,2,1,0:T(2,128)(2,1)S(1)}, bf16[2,1,192,2,768]{4,3,2,1,0:T(2,128)(2,1)S(1)}, u32[]{:S(2)}, u32[]{:S(2)}) %collective-permute-start.2) | collective-permute-done | bytes 1179680 | tf_op jit(solution)/shard_map/ppermute | solution.py:9
  257.8 23.1 %all-to-all-done = bf16[8,2,1,192,2,768]{5,4,3,1,2,0:T(2,128)(2,1)} async-done(((bf16[8,2,1,192,2,768]{5,4,3,1,2,0:T(2,128)(2,1)}), bf16[8,2,1,192,2,768]{5,4,3,1,2,0:T(2,128)(2,1)}, u32[]{:S(2)}, u32[]{:S(2)}) %all-to-all-start) | async-done | bytes 9437216 | tf_op jit(solution)/shard_map/all_to_all | solution.py:77
  280.9 6.2 stack.5
  287.1 6.5 all-to-all-start.1
  293.6 50.9 %collective-permute-start.3 = (bf16[2,192]{1,0:T(2,128)(2,1)S(1)}, bf16[2,192]{1,0:T(2,128)(2,1)S(1)}, u32[]{:S(2)}, u32[]{:S(2)}) collective-permute-start(bf16[2,192]{1,0:T(2,128)(2,1)S(1)} %copy-done.9), channel_id=1, source_target_pairs={{0,16},{8,24},{16,32},{24,40},{32,48},{40,56},{48,64},{56,72},{64,... | collective-permute-start | bytes 2312 | tf_op jit(solution)/shard_map/ppermute | solution.py:9
  344.5 0.6 fusion.169
  352.7 9.8 %fusion.168 = (bf16[1,8,192,2,768]{4,3,2,1,0:T(2,128)(2,1)}, bf16[1,8,192,2,768]{4,3,2,1,0:T(2,128)(2,1)}) fusion(bf16[2,8,192,2,768]{4,3,2,1,0:T(2,128)(2,1)} %param.21), kind=kLoop, calls=%fused_computation.155 | loop fusion | bytes 18874368 | tf_op jit(solution)/shard_map/slice | solution.py:85
  362.4 11.3 %squeeze.153 = bf16[8,192,1536]{2,1,0:T(8,128)(2,1)} reshape(bf16[1,8,192,2,768]{4,3,2,1,0:T(2,128)(2,1)} %get-tuple-element.382) | data formatting | bytes 9437184 | tf_op jit(solution)/shard_map/squeeze | solution.py:85
  373.7 11.3 %squeeze.149 = bf16[8,192,1536]{2,1,0:T(8,128)(2,1)} reshape(bf16[1,8,192,2,768]{4,3,2,1,0:T(2,128)(2,1)} %get-tuple-element.381) | data formatting | bytes 9437184 | tf_op jit(solution)/shard_map/squeeze | solution.py:85
  385.0 111.0 %collective-permute-done.1 = bf16[2,192]{1,0:T(2,128)(2,1)S(1)} collective-permute-done((bf16[2,192]{1,0:T(2,128)(2,1)S(1)}, bf16[2,192]{1,0:T(2,128)(2,1)S(1)}, u32[]{:S(2)}, u32[]{:S(2)}) %collective-permute-start.1) | collective-permute-done | bytes 800 | tf_op jit(solution)/shard_map/ppermute | solution.py:9
  496.0 20.9 %reshape_reshape.9 = bf16[2,8,192,1536]{3,2,0,1:T(8,128)(2,1)} reshape(bf16[2,8,1,192,2,768]{5,4,3,0,2,1:T(2,128)(2,1)} %bitcast.18) | data formatting | bytes 18874368 | tf_op jit(solution)/shard_map/reshape;reshape | solution.py:79
  516.9 8.6 %slice_negate_fusion.5 = (bf16[2,8,192,768]{3,2,0,1:T(8,128)(2,1)}, bf16[2,8,192,768]{3,2,0,1:T(8,128)(2,1)}) fusion(bf16[2,8,192,1536]{3,2,0,1:T(8,128)(2,1)} %reshape_reshape.9), kind=kLoop, calls=%fused_computation.131 | loop fusion | flops 2359296 | bytes 18874368 | tf_op jit(solution)/shard_map/neg | solution.py:26
  525.5 6.3 maximum_maximum_fusion
  531.8 6.9 dynamic-slice_bitcast_fusion.3
  538.7 21.8 %while.48 = (s32[]{:T(128)}, f32[192,384]{1,0:T(8,128)S(1)}, s32[2,2]{1,0:T(2,128)S(1)}, bf16[8,192,1536]{2,1,0:T(8,128)(2,1)}, bf16[8,384,1536]{2,1,0:T(8,128)(...) while((s32[]{:T(128)}, f32[192,384]{1,0:T(8,128)S(1)}, ...), condition=%wide.region_1.2_spmd.clone, body=%wide.region_0.1_spmd.clone.sunk | while | flops 511340544 | bytes 5900063 | solution.py:94
  538.7 0.7 fusion.210
  543.1 0.7 fusion.211
  545.2 2.0 fusion.212
  547.3 2.3 convolution_add_fusion.10
  549.6 0.7 fusion.210
  554.0 0.7 fusion.211
  556.1 2.0 fusion.212
  558.2 2.3 convolution_add_fusion.10
  560.5 0.7 copy-done.2
  561.3 1.0 copy.20
  562.2 21.8 %while.49 = (s32[]{:T(128)}, f32[192,384]{1,0:T(8,128)S(1)}, s32[2,2]{1,0:T(2,128)S(1)}, bf16[8,192,1536]{2,1,0:T(8,128)(2,1)}, bf16[8,384,1536]{2,1,0:T(8,128)(...) while((s32[]{:T(128)}, f32[192,384]{1,0:T(8,128)S(1)}, ...), condition=%wide.region_3.4_spmd.clone, body=%wide.region_2.3_spmd.clone.sunk | while | flops 511340544 | bytes 5900063 | solution.py:94
  562.2 0.6 fusion.216
  566.6 0.6 fusion.217
  568.7 2.0 fusion.218
  570.8 2.3 convolution_add_fusion.11
  573.1 0.6 fusion.216
  577.5 0.6 fusion.217
  579.5 2.0 fusion.218
  581.7 2.3 convolution_add_fusion.11
  584.0 0.7 copy-done.6
  584.7 20.9 %reshape_reshape.10 = bf16[2,8,192,1536]{3,2,0,1:T(8,128)(2,1)} reshape(bf16[2,8,1,192,2,768]{5,4,3,0,2,1:T(2,128)(2,1)} %bitcast.29) | data formatting | bytes 18874368 | tf_op jit(solution)/shard_map/reshape;reshape | solution.py:79
  605.6 8.6 %slice_negate_fusion.4 = (bf16[2,8,192,768]{3,2,0,1:T(8,128)(2,1)}, bf16[2,8,192,768]{3,2,0,1:T(8,128)(2,1)}) fusion(bf16[2,8,192,1536]{3,2,0,1:T(8,128)(2,1)} %reshape_reshape.10), kind=kLoop, calls=%fused_computation.130 | loop fusion | flops 2359296 | bytes 18874368 | tf_op jit(solution)/shard_map/neg | solution.py:26
  614.3 6.3 maximum_maximum_fusion.1
  620.6 6.7 dynamic-slice_bitcast_fusion
  627.3 21.7 %while.46 = (s32[]{:T(128)}, f32[192,384]{1,0:T(8,128)S(1)}, s32[2,2]{1,0:T(2,128)S(1)}, bf16[8,192,1536]{2,1,0:T(8,128)(2,1)}, bf16[8,384,1536]{2,1,0:T(8,128)(...) while((s32[]{:T(128)}, f32[192,384]{1,0:T(8,128)S(1)}, ...), condition=%wide.region_5.6_spmd, body=%wide.region_4.5_spmd.sunk | while | flops 511266816 | bytes 5900053 | solution.py:94
  627.3 0.6 fusion.198
  631.8 0.6 fusion.199
  633.8 2.0 fusion.200
  635.9 2.3 convolution_add_fusion.8
  638.2 0.6 fusion.198
  642.6 0.6 fusion.199
  644.6 2.0 fusion.200
  646.8 2.3 convolution_add_fusion.8
  649.2 21.6 %while.47 = (s32[]{:T(128)}, f32[192,384]{1,0:T(8,128)S(1)}, s32[2,2]{1,0:T(2,128)S(1)}, bf16[8,192,1536]{2,1,0:T(8,128)(2,1)}, bf16[8,384,1536]{2,1,0:T(8,128)(...) while((s32[]{:T(128)}, f32[192,384]{1,0:T(8,128)S(1)}, ...), condition=%wide.region_7.8_spmd, body=%wide.region_6.7_spmd.sunk | while | flops 511266816 | bytes 5900053 | solution.py:94
  649.2 0.6 fusion.204
  653.6 0.6 fusion.205
  655.6 2.0 fusion.206
  657.7 2.3 convolution_add_fusion.9
  660.0 0.6 fusion.204
  664.4 0.6 fusion.205
  666.4 2.0 fusion.206
  668.5 2.3 convolution_add_fusion.9
  671.7 25.5 %all_to_all.15 = f32[8,2,24,2,192]{4,3,2,1,0:T(2,128)S(1)} all-to-all(f32[8,2,24,2,192]{4,3,2,1,0:T(2,128)S(1)} %copy.6), channel_id=1, replica_groups=mesh['ka'=32,'occ'=8] {'occ'}, dimensions={0} | all-to-all | bytes 1179648 | tf_op jit(solution)/shard_map/all_to_all | solution.py:19
  697.2 1.0 reduce_sum.9
  (62 shorter events, 2.7 us)
Async XLA Ops:
  2.1 45.5 %collective-permute-start = (bf16[2,1,192,2,768]{4,3,2,1,0:T(2,128)(2,1)S(1)}, bf16[2,1,192,2,768]{4,3,2,1,0:T(2,128)(2,1)S(1)}, u32[]{:S(2)}, u32[]{:S(2)}) collective-permute-start(bf16[2,1,192,2,768]{4,3,2,1,0:T(2,128)(2,1)S(1)} %constant_dynamic-slice_fusion.8), channel_id=1, source_target_pairs={{0,8},{8,16},{16,24},{24,32},{32,40},{40,48},{48,56},{56,64},{64,7... | collective-permute-start | bytes 3538952 | tf_op jit(solution)/shard_map/ppermute | solution.py:9
  53.8 227.0 %all-to-all-start = ((bf16[8,2,1,192,2,768]{5,4,3,1,2,0:T(2,128)(2,1)}), bf16[8,2,1,192,2,768]{5,4,3,1,2,0:T(2,128)(2,1)}, u32[]{:S(2)}, u32[]{:S(2)}) async-start(bf16[8,2,1,192,2,768]{5,4,3,1,2,0:T(2,128)(2,1)} %stack.4), calls=%async_computation | async-start | bytes 18874368 | tf_op jit(solution)/shard_map/all_to_all | solution.py:77
  75.8 181.9 %collective-permute-start.2 = (bf16[2,1,192,2,768]{4,3,2,1,0:T(2,128)(2,1)S(1)}, bf16[2,1,192,2,768]{4,3,2,1,0:T(2,128)(2,1)S(1)}, u32[]{:S(2)}, u32[]{:S(2)}) collective-permute-start(bf16[2,1,192,2,768]{4,3,2,1,0:T(2,128)(2,1)S(1)} %constant_dynamic-slice_fusion.8), channel_id=1, source_target_pairs={{0,16},{8,24},{16,32},{24,40},{32,48},{40,56},{48,64},{56,72},{64,... | collective-permute-start | bytes 3538952 | tf_op jit(solution)/shard_map/ppermute | solution.py:9
  287.0 6.5 copy-start.9
  287.0 57.5 %copy-start.8 = (s32[2,2]{1,0:T(2,128)S(1)}, s32[2,2]{1,0:T(2,128)}, u32[]{:S(2)}) copy-start(s32[2,2]{1,0:T(2,128)} %param.24) | copy-start | bytes 52
  287.0 65.6 %copy-start.10 = (s32[2,2,2]{2,1,0:T(2,128)S(1)}, s32[2,2,2]{2,1,0:T(2,128)}, u32[]{:S(2)}) copy-start(s32[2,2,2]{2,1,0:T(2,128)} %param.25) | copy-start | bytes 100
  287.1 297.0 %all-to-all-start.1 = ((bf16[8,2,1,192,2,768]{5,4,3,1,2,0:T(2,128)(2,1)}), bf16[8,2,1,192,2,768]{5,4,3,1,2,0:T(2,128)(2,1)}, u32[]{:S(2)}, u32[]{:S(2)}) async-start(bf16[8,2,1,192,2,768]{5,4,3,1,2,0:T(2,128)(2,1)} %stack.5), calls=%async_computation.1 | async-start | bytes 18874368 | tf_op jit(solution)/shard_map/all_to_all | solution.py:77
  293.6 202.4 %collective-permute-start.1 = (bf16[2,192]{1,0:T(2,128)(2,1)S(1)}, bf16[2,192]{1,0:T(2,128)(2,1)S(1)}, u32[]{:S(2)}, u32[]{:S(2)}) collective-permute-start(bf16[2,192]{1,0:T(2,128)(2,1)S(1)} %copy-done.9), channel_id=1, source_target_pairs={{0,8},{8,16},{16,24},{24,32},{32,40},{40,48},{48,56},{56,64},{64,7... | collective-permute-start | bytes 2312 | tf_op jit(solution)/shard_map/ppermute | solution.py:9
  293.6 202.4 %collective-permute-start.3 = (bf16[2,192]{1,0:T(2,128)(2,1)S(1)}, bf16[2,192]{1,0:T(2,128)(2,1)S(1)}, u32[]{:S(2)}, u32[]{:S(2)}) collective-permute-start(bf16[2,192]{1,0:T(2,128)(2,1)S(1)} %copy-done.9), channel_id=1, source_target_pairs={{0,16},{8,24},{16,32},{24,40},{32,48},{40,56},{48,64},{56,72},{64,... | collective-permute-start | bytes 2312 | tf_op jit(solution)/shard_map/ppermute | solution.py:9
  516.9 8.7 %copy-start = (bf16[2,8,192,1536]{3,2,0,1:T(8,128)(2,1)S(1)}, bf16[2,8,192,1536]{3,2,0,1:T(8,128)(2,1)}, u32[]{:S(2)}) copy-start(bf16[2,8,192,1536]{3,2,0,1:T(8,128)(2,1)} %reshape_reshape.9) | copy-start | bytes 28311556
  531.8 6.9 copy-start.4
  538.7 23.5 %copy-start.5 = (f32[192,384]{1,0:T(8,128)S(1)}, f32[192,384]{1,0:T(8,128)}, u32[]{:S(2)}) copy-start(f32[192,384]{1,0:T(8,128)} %custom-call.1) | copy-start | bytes 884740
  560.5 0.7 copy-start.2
  584.0 0.7 copy-start.6
  605.6 8.7 %copy-start.1 = (bf16[2,8,192,1536]{3,2,0,1:T(8,128)(2,1)S(1)}, bf16[2,8,192,1536]{3,2,0,1:T(8,128)(2,1)}, u32[]{:S(2)}) copy-start(bf16[2,8,192,1536]{3,2,0,1:T(8,128)(2,1)} %reshape_reshape.10) | copy-start | bytes 28311556
  627.3 21.7 %copy-start.3 = (f32[192,384]{1,0:T(8,128)S(1)}, f32[192,384]{1,0:T(8,128)}, u32[]{:S(2)}) copy-start(f32[192,384]{1,0:T(8,128)} %copy-done.2) | copy-start | bytes 884740
  627.3 21.7 %copy-start.7 = (f32[192,384]{1,0:T(8,128)S(1)}, f32[192,384]{1,0:T(8,128)}, u32[]{:S(2)}) copy-start(f32[192,384]{1,0:T(8,128)} %copy-done.6) | copy-start | bytes 884740
